TPU v7x, 32 devices: a whole 2x2x4 slice. The times are simulated.
32 devices in a mesh: grid: 8 (over y, x, core), sub: 4 (over z).
Axes of the slice: x: 2, y: 2, z: 4, core: 2. Of those that a mesh axis runs over, the one named last changes fastest.
Arguments:
- grid_x: bfloat16 [65536, 512], P(('grid', 'sub')), may hold values from -6 to 6
- mesh_h: bfloat16 [2048, 512], P(('grid', 'sub')), may hold values from -6 to 6
- gain_grid: float32 [512], replicated, may hold values from 0.1 to 1.9
- gain_mesh: float32 [512], replicated, may hold values from 0.1 to 1.9
- w_query: bfloat16 [512, 512], replicated, may hold values from -0.25 to 0.25
- w_key: bfloat16 [512, 512], replicated, may hold values from -0.25 to 0.25
- w_value: bfloat16 [512, 512], replicated, may hold values from -0.25 to 0.25
- w_out: bfloat16 [512, 512], replicated, may hold values from -0.25 to 0.25
- edge_bias: float32 [2048, 384], P(('grid', 'sub')), may hold values from -9 to 300
- neighbours: int32 [2048, 96], P(('grid', 'sub')), may hold values from 0 to 767, as said below
- valid: int32 [2048, 96], P(('grid', 'sub')), may hold values from 0 to 1, as said below
- send_rows: int32 [32, 3, 4, 64], P(('grid', 'sub')), may hold values from 0 to 2047, as said below
- out_grad: bfloat16 [2048, 512], P(('grid', 'sub')), may hold values from -24 to 24
Outputs:
- mesh_out: bfloat16 [2048, 512], P(('grid', 'sub'))
- mesh_grad: bfloat16 [2048, 512], P(('grid', 'sub'))
- grid_grad: bfloat16 [65536, 512], P(('grid', 'sub'))
- weight_grads: float32 [4, 512, 512], replicated
Inputs may be any that keep to these rules, and one draw needn't show every extreme that they name: `send_rows`: for each source device, slab offset and destination sub index the 64 local rows are distinct; rows sent to the slab below (o = 0) lie in the lower half of the device's 2048 rows, rows sent to the slab above (o = 2) in the upper half. `neighbours`: a slot (o * 4 + s) * 64 + t names row t of what device s of slab g - o + 1 sends to the node's device; slots of slabs outside the grid are never named; the 96 entries of a node are distinct; some slots are named by no node. The first two edges of every node are valid.
All inputs are finite; a program needn't handle non-finite values.
Results may differ from a plain program's by a relative error of at most 0.009.
Values may be sent and summed in bfloat16 or wider, within the bound.
A program may use at most 128 MiB of HBM per device.

v0:
```python
import jax
import jax.numpy as jnp
from jax import lax
from jax.sharding import PartitionSpec as P

EPSILON = 1e-06
NEG_FILL = -1e30


def from_behind(block, axis, distance):
    devices = range(lax.axis_size(axis))
    route = [(i - distance, i) for i in devices if i - distance in devices]
    return lax.ppermute(block, axis, route)


def normalize(values_in, gain_row):
    widened = values_in.astype(jnp.float32)
    factor = lax.rsqrt(jnp.mean(widened * widened, axis=-1, keepdims=True) + EPSILON)
    return (widened, factor, (widened * factor * gain_row).astype(jnp.bfloat16))


def normalize_back(widened, factor, gain_row, upstream):
    scaled = gain_row * upstream
    inner_mean = jnp.mean(widened * scaled, axis=-1, keepdims=True)
    return factor * scaled - widened * factor**3 * inner_mean


def shards(
    grid_x,
    mesh_h,
    gain_grid,
    gain_mesh,
    w_query,
    w_key,
    w_value,
    w_out,
    edge_bias,
    neighbours,
    valid,
    send_rows,
    out_grad,
):
    point_count, model_width = grid_x.shape
    node_count = mesh_h.shape[0]
    sub_count = send_rows.shape[2]
    slots_per = send_rows.shape[3]
    block = sub_count * slots_per
    slot_count = 3 * block
    fanout = neighbours.shape[1]
    head_count = edge_bias.shape[1] // fanout
    head_width = model_width // head_count
    logit_scale = head_width ** (-0.5)
    w_pair = jnp.concatenate([w_key, w_value], axis=1)
    grid_wide, grid_factor, grid_normed = normalize(grid_x, gain_grid)
    flat_rows = send_rows[0].reshape(slot_count)
    send_match = flat_rows[:, None] == jnp.arange(point_count, dtype=jnp.int32)[None, :]
    send_onehot = send_match.astype(jnp.bfloat16)
    sent_normed = jnp.dot(send_onehot, grid_normed, preferred_element_type=jnp.float32).astype(
        jnp.bfloat16
    )
    packet = sent_normed.reshape(3, sub_count, slots_per, model_width)
    packet_width = packet.shape[3]
    mixed = lax.all_to_all(packet, "sub", split_axis=1, concat_axis=1, tiled=True).reshape(
        3, block, packet_width
    )
    pieces = []
    for offset in (0, 1, 2):
        piece = mixed[offset]
        if offset != 1:
            piece = from_behind(piece, "grid", offset - 1)
        pieces.append(piece)
    arrived = jnp.concatenate(pieces, axis=0)
    recv_pair = jnp.dot(arrived, w_pair, preferred_element_type=jnp.float32).astype(jnp.bfloat16)
    slot_onehot = (
        neighbours[:, :, None] == jnp.arange(slot_count, dtype=jnp.int32)[None, None, :]
    ).astype(jnp.bfloat16)
    edge_pair = jnp.einsum(
        "gjc,ce->gje", slot_onehot, recv_pair, preferred_element_type=jnp.float32
    ).astype(jnp.bfloat16)
    edge_keys = edge_pair[:, :, :model_width].reshape(node_count, fanout, head_count, head_width)
    edge_values = edge_pair[:, :, model_width:].reshape(node_count, fanout, head_count, head_width)
    mesh_wide, mesh_factor, mesh_normed = normalize(mesh_h, gain_mesh)
    queries = (
        jnp.dot(mesh_normed, w_query, preferred_element_type=jnp.float32) * logit_scale
    ).astype(jnp.bfloat16)
    query_head_rows = queries.reshape(node_count, head_count, head_width)
    score_matrix = jnp.einsum(
        "gip,gjip->gij", query_head_rows, edge_keys, preferred_element_type=jnp.float32
    ) + edge_bias.reshape(node_count, head_count, fanout)
    live_mask = (valid == 1)[:, None, :]
    row_peak = jnp.max(jnp.where(live_mask, score_matrix, NEG_FILL), axis=2, keepdims=True)
    exp_terms = jnp.exp(jnp.where(live_mask, score_matrix - row_peak, NEG_FILL))
    attn_probs = exp_terms / jnp.sum(exp_terms, axis=2, keepdims=True)
    probabilities_batch = attn_probs.astype(jnp.bfloat16)
    attended_rows = (
        jnp.einsum(
            "gij,gjik->gik", probabilities_batch, edge_values, preferred_element_type=jnp.float32
        )
        .reshape(node_count, model_width)
        .astype(jnp.bfloat16)
    )
    mesh_out = (
        mesh_wide + jnp.dot(attended_rows, w_out, preferred_element_type=jnp.float32)
    ).astype(jnp.bfloat16)
    grad_wo = jnp.einsum("md,me->de", attended_rows, out_grad, preferred_element_type=jnp.float32)
    att_grad = jnp.einsum("me,de->md", out_grad, w_out, preferred_element_type=jnp.float32).astype(
        jnp.bfloat16
    )
    head_gradient = att_grad.reshape(node_count, head_count, head_width)
    probability_gradient = jnp.einsum(
        "gip,gjip->gij", head_gradient, edge_values, preferred_element_type=jnp.float32
    )
    score_gradient = (
        attn_probs
        * (probability_gradient - jnp.sum(attn_probs * probability_gradient, axis=2, keepdims=True))
    ).astype(jnp.bfloat16)
    query_gradient = (
        (
            jnp.einsum(
                "gij,gjik->gik", score_gradient, edge_keys, preferred_element_type=jnp.float32
            )
            * logit_scale
        )
        .reshape(node_count, model_width)
        .astype(jnp.bfloat16)
    )
    dense_score_gradient = jnp.einsum(
        "gij,gjc->gic", score_gradient, slot_onehot, preferred_element_type=jnp.float32
    ).astype(jnp.bfloat16)
    dense_probabilities = jnp.einsum(
        "gij,gjc->gic", probabilities_batch, slot_onehot, preferred_element_type=jnp.float32
    ).astype(jnp.bfloat16)
    key_part = jnp.einsum(
        "uza,uzt->azt", dense_score_gradient, query_head_rows, preferred_element_type=jnp.float32
    ).reshape(slot_count, model_width)
    value_part = jnp.einsum(
        "uza,uzt->azt", dense_probabilities, head_gradient, preferred_element_type=jnp.float32
    ).reshape(slot_count, model_width)
    back_packet = (
        jnp.concatenate([key_part, value_part], axis=1)
        .astype(jnp.bfloat16)
        .reshape(3, block, 2 * model_width)
    )
    home_pieces = []
    for offset in (0, 1, 2):
        piece = back_packet[offset]
        if offset != 1:
            piece = from_behind(piece, "grid", 1 - offset)
        home_pieces.append(piece)
    home = jnp.stack(home_pieces)
    home = home.reshape(3, sub_count, slots_per, 2 * model_width)
    returned = lax.all_to_all(home, "sub", split_axis=1, concat_axis=1, tiled=True).reshape(
        slot_count, 2 * model_width
    )
    pair_grads = jnp.einsum("sd,se->de", sent_normed, returned, preferred_element_type=jnp.float32)
    slot_back = jnp.einsum("se,de->sd", returned, w_pair, preferred_element_type=jnp.float32)
    normed_grad = jnp.einsum(
        "sp,sd->pd",
        send_match.astype(jnp.float32),
        slot_back,
        precision=lax.Precision.HIGHEST,
        preferred_element_type=jnp.float32,
    )
    grid_grad = normalize_back(grid_wide, grid_factor, gain_grid, normed_grad).astype(jnp.bfloat16)
    grad_wq = jnp.einsum(
        "md,me->de", mesh_normed, query_gradient, preferred_element_type=jnp.float32
    )
    mesh_normed_grad = jnp.einsum(
        "me,de->md", query_gradient, w_query, preferred_element_type=jnp.float32
    )
    mesh_grad = (
        out_grad.astype(jnp.float32)
        + normalize_back(mesh_wide, mesh_factor, gain_mesh, mesh_normed_grad)
    ).astype(jnp.bfloat16)
    local_grads = jnp.stack(
        [grad_wq, pair_grads[:, :model_width], pair_grads[:, model_width:], grad_wo]
    )
    weight_grads = lax.psum(local_grads, ("grid", "sub"))
    return (mesh_out, mesh_grad, grid_grad, weight_grads)


def solution(mesh):
    in_specs = (
        P(("grid", "sub"), None),
        P(("grid", "sub"), None),
        P(),
        P(),
        P(),
        P(),
        P(),
        P(),
        P(("grid", "sub"), None),
        P(("grid", "sub"), None),
        P(("grid", "sub"), None),
        P(("grid", "sub"), None, None, None),
        P(("grid", "sub"), None),
    )
    out_specs = (P(("grid", "sub"), None), P(("grid", "sub"), None), P(("grid", "sub"), None), P())
    return jax.shard_map(shards, mesh=mesh, in_specs=in_specs, out_specs=out_specs, check_vma=False)
```

profile of v0, /device:TPU:0, one launch (start us, length us, event | category | flops | bytes accessed | tf_op | source)
XLA Modules:
  0.0 303.4 jit_solution(8482572767754308976)
XLA Ops:
  7.2 3.0 copy.27
  10.2 0.5 fusion.22
  10.8 2.0 fusion.35
  12.8 0.9 copy-done.9
  13.7 0.9 copy.28
  14.6 6.3 %all-to-all-start = ((bf16[3,4,64,512]{3,2,0,1:T(8,128)(2,1)}), bf16[3,4,64,512]{3,2,0,1:T(8,128)(2,1)S(1)}, u32[]{:S(2)}, u32[]{:S(2)}) async-start(bf16[3,4,64,512]{3,2,0,1:T(8,128)(2,1)} %copy.28), calls=%async_computation | async-start | bytes 1572864 | tf_op jit(solution)/shard_map/all_to_all | solution.py:63
  21.1 1.9 constant_dynamic-update-slice_fusion.1
  23.0 0.5 multiply_multiply_fusion.1
  23.5 0.3 convolution_convert_fusion.3
  24.1 17.0 %all-to-all-done = bf16[3,4,64,512]{3,2,0,1:T(8,128)(2,1)S(1)} async-done(((bf16[3,4,64,512]{3,2,0,1:T(8,128)(2,1)}), bf16[3,4,64,512]{3,2,0,1:T(8,128)(2,1)S(1)}, u32[]{:S(2)}, u32[]{:S(2)}) %all-to-all-start) | async-done | bytes 786464 | tf_op jit(solution)/shard_map/all_to_all | solution.py:63
  41.1 1.3 collective-permute-start
  42.4 3.2 %collective-permute-start.1 = (bf16[256,512]{1,0:T(8,128)(2,1)S(1)}, bf16[256,512]{1,0:T(8,128)(2,1)S(1)}, u32[]{:S(2)}, u32[]{:S(2)}) collective-permute-start(bf16[256,512]{1,0:T(8,128)(2,1)S(1)} %bitcast.119), channel_id=1, source_target_pairs={{0,4},{4,8},{8,12},{12,16},{16,20},{20,24},{24,28},{1,5},{5,9},{9,... | collective-permute-start | bytes 786440 | tf_op jit(solution)/shard_map/ppermute | solution.py:13
  45.7 0.9 constant_dynamic-update-slice_fusion
  46.8 2.2 fusion.123
  49.0 11.4 %fusion.7 = bf16[64,96,1024]{2,1,0:T(8,128)(2,1)S(1)} fusion(s32[64,96]{1,0:T(8,128)} %param.22, bf16[768,1024,1]{1,0,2:T(8,128)(2,1)S(1)} %fusion.123), kind=kOutput, calls=%fused_computation.12 | convolution fusion | flops 9674686464 | bytes 14180352 | tf_op jit(solution)/shard_map/gjc,ce->gje/dot_general | solution.py:77
  60.5 3.7 %slice_bitcast_fusion.1 = (bf16[64,12,4,8,128]{4,3,2,1,0:T(8,128)(2,1)S(1)}, bf16[64,12,4,8,128]{4,3,2,1,0:T(8,128)(2,1)S(1)}) fusion(bf16[64,96,1024]{2,1,0:T(8,128)(2,1)S(1)} %fusion.7), kind=kLoop, calls=%fused_computation.22 | loop fusion | bytes 25165824
  64.2 3.3 %fusion.14 = f32[64,4,1,96]{3,2,1,0:T(1,128)S(1)} fusion(bf16[64,4,128,1]{2,3,1,0:T(2,128)(2,1)S(1)} %reshape.124, bf16[64,12,4,8,128]{4,3,2,1,0:T(8,128)(2,1)S(1)} %get-tuple-element.16), kind=kOutput, calls=%fused_computation.19 | convolution fusion | flops 6291456 | bytes 6455296 | tf_op jit(solution)/shard_map/gip,gjip->gij/dot_general | solution.py:87
  67.6 3.3 %fusion.8 = f32[64,4,1,96]{3,2,1,0:T(1,128)S(1)} fusion(bf16[64,4,128,1]{2,3,1,0:T(2,128)(2,1)S(1)} %reshape.126, bf16[64,12,4,8,128]{4,3,2,1,0:T(8,128)(2,1)S(1)} %get-tuple-element.17), kind=kOutput, calls=%fused_computation.13 | convolution fusion | flops 6291456 | bytes 6455296 | tf_op jit(solution)/shard_map/gip,gjip->gij/dot_general | solution.py:110
  71.2 3.6 %fusion.39 = bf16[64,4,768]{2,1,0:T(4,128)(2,1)S(1)} fusion(s32[64,96]{1,0:T(8,128)S(1)} %copy-done.29, f32[64,4,96]{2,1,0:T(4,128)S(1)} %get-tuple-element.33, f32[64,4]{1,0:T(8,128)S(1)} %get-tuple-element.32), kind=kOutput, calls=%fused_computation.55 | convolution fusion | flops 42713088 | bytes 517120 | tf_op jit(solution)/shard_map/gij,gjc->gic/dot_general | solution.py:130
  75.0 0.8 multiply_convert_fusion.1
  75.8 3.5 %fusion.38 = bf16[64,4,768]{2,1,0:T(4,128)(2,1)S(1)} fusion(bf16[64,4,96]{2,1,0:T(4,128)(2,1)S(1)} %get-tuple-element.26, s32[64,96]{1,0:T(8,128)S(1)} %copy-done.29), kind=kOutput, calls=%fused_computation.54 | convolution fusion | flops 42663936 | bytes 466944 | tf_op jit(solution)/shard_map/gij,gjc->gic/dot_general | solution.py:127
  79.3 0.4 convolution_convert_fusion.2
  79.8 0.3 copy.33
  80.1 0.4 convolution_convert_fusion.1
  81.0 5.0 %collective-permute-start.2 = (bf16[256,1024]{1,0:T(8,128)(2,1)S(1)}, bf16[256,1024]{1,0:T(8,128)(2,1)S(1)}, u32[]{:S(2)}, u32[]{:S(2)}) collective-permute-start(bf16[256,1024]{1,0:T(8,128)(2,1)S(1)} %get-tuple-element.20), channel_id=1, source_target_pairs={{0,4},{4,8},{8,12},{12,16},{16,20},{20,24},{24,28},{1,5},{5,9},{9,... | collective-permute-start | bytes 1572872 | tf_op jit(solution)/shard_map/ppermute | solution.py:13
  86.0 1.3 collective-permute-start.3
  87.5 4.3 %collective-permute-done.3 = bf16[256,1024]{1,0:T(8,128)(2,1)S(1)} collective-permute-done((bf16[256,1024]{1,0:T(8,128)(2,1)S(1)}, bf16[256,1024]{1,0:T(8,128)(2,1)S(1)}, u32[]{:S(2)}, u32[]{:S(2)}) %collective-permute-start.3) | collective-permute-done | bytes 524320 | tf_op jit(solution)/shard_map/ppermute | solution.py:13
  91.9 1.3 copy.35
  93.2 4.4 %all-to-all-start.1 = ((bf16[3,4,64,1024]{3,2,0,1:T(8,128)(2,1)}), bf16[3,4,64,1024]{3,2,0,1:T(8,128)(2,1)}, u32[]{:S(2)}, u32[]{:S(2)}) async-start(bf16[3,4,64,1024]{3,2,0,1:T(8,128)(2,1)} %copy.35), calls=%async_computation.1 | async-start | bytes 3145728 | tf_op jit(solution)/shard_map/all_to_all | solution.py:152
  97.9 4.7 %fusion.10 = f32[64,4,1,128]{3,2,1,0:T(1,128)S(1)} fusion(bf16[64,12,4,8,128]{4,3,2,1,0:T(8,128)(2,1)} %copy-done.2, bf16[64,4,96,1]{2,1,0,3:T(4,128)(2,1)S(1)} %copy-done.16), kind=kOutput, calls=%fused_computation.15 | convolution fusion | flops 6291456 | bytes 6471680 | tf_op jit(solution)/shard_map/gij,gjik->gik/dot_general | solution.py:96
  102.6 1.3 convolution_bitcast_fusion
  103.9 1.7 fusion.12
  105.7 0.4 convolution_bitcast_fusion.1
  106.1 0.4 fusion.67
  106.5 24.3 %all-to-all-done.1 = bf16[3,4,64,1024]{3,2,0,1:T(8,128)(2,1)} async-done(((bf16[3,4,64,1024]{3,2,0,1:T(8,128)(2,1)}), bf16[3,4,64,1024]{3,2,0,1:T(8,128)(2,1)}, u32[]{:S(2)}, u32[]{:S(2)}) %all-to-all-start.1) | async-done | bytes 1572896 | tf_op jit(solution)/shard_map/all_to_all | solution.py:152
  130.8 1.6 copy.36
  132.4 1.0 fusion.94
  133.6 0.6 copy-done.5
  134.2 2.5 pad_maximum_fusion
  136.7 0.6 copy-done.23
  137.3 0.7 fusion.66
  138.0 0.8 fusion.44
  138.8 2.7 fusion.93
  141.6 6.1 %fusion.28 = (f32[2048]{0:T(1024)S(1)}, f32[2048,512]{0,1:T(8,128)S(1)}) fusion(bf16[2048,512]{0,1:T(8,128)(2,1)S(1)} %copy-done.4, f32[512]{0:T(512)S(1)} %copy-done.27, f32[768,512]{1,0:T(8,128)S(1)} %fusion.93, s32[768]{0:T(1024)S(1)} %copy-done.25), kind=kOutput, calls=%fused_computation.36 | convolution fusion | flops 9669441536 | bytes 7877632 | tf_op jit(solution)/shard_map/sp,sd->pd/dot_general | solution.py:157
  147.7 2.6 fusion.27
  150.3 3.9 %copy.37 = bf16[2048,512]{1,0:T(8,128)(2,1)} copy(bf16[2048,512]{0,1:T(8,128)(2,1)} %fusion.27) | data formatting | bytes 4194304
  154.2 137.7 %all-reduce.2.cloned.1.call-done = f32[4,512,512]{2,1,0:T(8,128)} async-done(((f32[4,512,512]{2,1,0:T(8,128)}), f32[4,512,512]{2,1,0:T(8,128)}) %all-reduce.2.cloned.1.call-update) | async-done | bytes 4194320 | tf_op jit(solution)/shard_map/psum | solution.py:178
  291.9 4.6 %copy.106 = f32[4,512,512]{2,1,0:T(8,128)} copy(f32[4,512,512]{2,1,0:T(8,128)} %all-reduce.2.cloned.1.call-done) | data formatting | bytes 8388608
  (86 shorter events, 2.7 us)
Async XLA Ops:
  7.2 16.6 %copy-start = (bf16[512,512]{1,0:T(8,128)(2,1)S(1)}, bf16[512,512]{1,0:T(8,128)(2,1)}, u32[]{:S(2)}) copy-start(bf16[512,512]{1,0:T(8,128)(2,1)} %param.17) | copy-start | bytes 1572868
  7.2 3.5 %copy-start.20 = (s32[1,3,4,64]{3,2,1,0:T(4,128)S(1)}, s32[1,3,4,64]{3,2,1,0:T(4,128)}, u32[]{:S(2)}) copy-start(s32[1,3,4,64]{3,2,1,0:T(4,128)} %param.24) | copy-start | bytes 9220
  7.2 3.6 %copy-start.26 = (f32[512]{0:T(512)S(1)}, f32[512]{0:T(512)}, u32[]{:S(2)}) copy-start(f32[512]{0:T(512)} %param.15) | copy-start | bytes 6148
  10.2 2.5 copy-start.3
  10.8 2.0 copy-start.24
  10.8 10.2 %copy-start.6 = (bf16[64,512]{1,0:T(8,128)(2,1)S(1)}, bf16[64,512]{1,0:T(8,128)(2,1)}, u32[]{:S(2)}) copy-start(bf16[64,512]{1,0:T(8,128)(2,1)} %param.14) | copy-start | bytes 196612
  12.7 0.9 copy-start.9
  12.8 10.7 %copy-start.7 = (bf16[512,512]{1,0:T(8,128)(2,1)S(1)}, bf16[512,512]{1,0:T(8,128)(2,1)}, u32[]{:S(2)}) copy-start(bf16[512,512]{1,0:T(8,128)(2,1)} %param.20) | copy-start | bytes 1572868
  12.8 10.7 %copy-start.11 = (bf16[64,512]{1,0:T(8,128)(2,1)S(1)}, bf16[64,512]{1,0:T(8,128)(2,1)}, u32[]{:S(2)}) copy-start(bf16[64,512]{1,0:T(8,128)(2,1)} %param.25) | copy-start | bytes 196612
  13.7 10.1 %copy-start.18 = (f32[512]{0:T(512)S(1)}, f32[512]{0:T(512)}, u32[]{:S(2)}) copy-start(f32[512]{0:T(512)} %param.16) | copy-start | bytes 6148
  13.7 32.0 %copy-start.12 = (bf16[512,512]{1,0:T(8,128)(2,1)S(1)}, bf16[512,512]{1,0:T(8,128)(2,1)}, u32[]{:S(2)}) copy-start(bf16[512,512]{1,0:T(8,128)(2,1)} %param.19) | copy-start | bytes 1572868
  13.7 32.9 %copy-start.13 = (f32[64,384]{1,0:T(8,128)S(1)}, f32[64,384]{1,0:T(8,128)}, u32[]{:S(2)}) copy-start(f32[64,384]{1,0:T(8,128)} %param.21) | copy-start | bytes 294916
  13.7 33.1 %copy-start.17 = (s32[64,96]{1,0:T(8,128)S(1)}, s32[64,96]{1,0:T(8,128)}, u32[]{:S(2)}) copy-start(s32[64,96]{1,0:T(8,128)} %param.23) | copy-start | bytes 73732
  14.6 26.5 %all-to-all-start = ((bf16[3,4,64,512]{3,2,0,1:T(8,128)(2,1)}), bf16[3,4,64,512]{3,2,0,1:T(8,128)(2,1)S(1)}, u32[]{:S(2)}, u32[]{:S(2)}) async-start(bf16[3,4,64,512]{3,2,0,1:T(8,128)(2,1)} %copy.28), calls=%async_computation | async-start | bytes 1572864 | tf_op jit(solution)/shard_map/all_to_all | solution.py:63
  23.5 0.6 copy-start.21
  41.1 5.7 %collective-permute-start = (bf16[256,512]{1,0:T(8,128)(2,1)S(1)}, bf16[256,512]{1,0:T(8,128)(2,1)S(1)}, u32[]{:S(2)}, u32[]{:S(2)}) collective-permute-start(bf16[256,512]{1,0:T(8,128)(2,1)S(1)} %bitcast.120), channel_id=1, source_target_pairs={{4,0},{8,4},{12,8},{16,12},{20,16},{24,20},{28,24},{5,1},{9,5},{13... | collective-permute-start | bytes 786440 | tf_op jit(solution)/shard_map/ppermute | solution.py:13
  42.4 4.4 %collective-permute-start.1 = (bf16[256,512]{1,0:T(8,128)(2,1)S(1)}, bf16[256,512]{1,0:T(8,128)(2,1)S(1)}, u32[]{:S(2)}, u32[]{:S(2)}) collective-permute-start(bf16[256,512]{1,0:T(8,128)(2,1)S(1)} %bitcast.119), channel_id=1, source_target_pairs={{0,4},{4,8},{8,12},{12,16},{16,20},{20,24},{24,28},{1,5},{5,9},{9,... | collective-permute-start | bytes 786440 | tf_op jit(solution)/shard_map/ppermute | solution.py:13
  64.2 6.7 %copy-start.1 = (bf16[64,12,4,8,128]{4,3,2,1,0:T(8,128)(2,1)}, bf16[64,12,4,8,128]{4,3,2,1,0:T(8,128)(2,1)S(1)}, u32[]{:S(2)}) copy-start(bf16[64,12,4,8,128]{4,3,2,1,0:T(8,128)(2,1)S(1)} %get-tuple-element.16) | copy-start | bytes 18874372
  64.2 6.7 %copy-start.2 = (bf16[64,12,4,8,128]{4,3,2,1,0:T(8,128)(2,1)}, bf16[64,12,4,8,128]{4,3,2,1,0:T(8,128)(2,1)S(1)}, u32[]{:S(2)}) copy-start(bf16[64,12,4,8,128]{4,3,2,1,0:T(8,128)(2,1)S(1)} %get-tuple-element.17) | copy-start | bytes 18874372
  67.6 3.6 %copy-start.29 = (s32[64,96]{1,0:T(8,128)S(1)}, s32[64,96]{1,0:T(8,128)}, u32[]{:S(2)}) copy-start(s32[64,96]{1,0:T(8,128)} %param.22) | copy-start | bytes 73732
  75.8 4.0 %copy-start.14 = (bf16[64,4,96]{2,1,0:T(4,128)(2,1)}, bf16[64,4,96]{2,1,0:T(4,128)(2,1)S(1)}, u32[]{:S(2)}) copy-start(bf16[64,4,96]{2,1,0:T(4,128)(2,1)S(1)} %get-tuple-element.26) | copy-start | bytes 147460
  81.0 6.5 %collective-permute-start.2 = (bf16[256,1024]{1,0:T(8,128)(2,1)S(1)}, bf16[256,1024]{1,0:T(8,128)(2,1)S(1)}, u32[]{:S(2)}, u32[]{:S(2)}) collective-permute-start(bf16[256,1024]{1,0:T(8,128)(2,1)S(1)} %get-tuple-element.20), channel_id=1, source_target_pairs={{0,4},{4,8},{8,12},{12,16},{16,20},{20,24},{24,28},{1,5},{5,9},{9,... | collective-permute-start | bytes 1572872 | tf_op jit(solution)/shard_map/ppermute | solution.py:13
  86.0 5.8 %collective-permute-start.3 = (bf16[256,1024]{1,0:T(8,128)(2,1)S(1)}, bf16[256,1024]{1,0:T(8,128)(2,1)S(1)}, u32[]{:S(2)}, u32[]{:S(2)}) collective-permute-start(bf16[256,1024]{1,0:T(8,128)(2,1)S(1)} %get-tuple-element.21), channel_id=1, source_target_pairs={{4,0},{8,4},{12,8},{16,12},{20,16},{24,20},{28,24},{5,1},{9,5},{13... | collective-permute-start | bytes 1572872 | tf_op jit(solution)/shard_map/ppermute | solution.py:13
  91.7 6.1 %copy-start.16 = (bf16[64,4,96,1]{2,1,0,3:T(4,128)(2,1)S(1)}, bf16[64,4,96,1]{2,1,0,3:T(4,128)(2,1)}, u32[]{:S(2)}) copy-start(bf16[64,4,96,1]{2,1,0,3:T(4,128)(2,1)} %get-tuple-element.27) | copy-start | bytes 147460
  91.9 12.0 %slice-start = ((s8[6291456]{0:T(1024)(128)(4,1)}), s8[2097152]{0:T(1024)(128)(4,1)S(1)}, s32[]{:S(2)}) async-start(s8[6291456]{0:T(1024)(128)(4,1)} %bitcast.102), calls=%async_computation.3 | async-start | bytes 4194304
  93.2 37.6 %all-to-all-start.1 = ((bf16[3,4,64,1024]{3,2,0,1:T(8,128)(2,1)}), bf16[3,4,64,1024]{3,2,0,1:T(8,128)(2,1)}, u32[]{:S(2)}, u32[]{:S(2)}) async-start(bf16[3,4,64,1024]{3,2,0,1:T(8,128)(2,1)} %copy.35), calls=%async_computation.1 | async-start | bytes 3145728 | tf_op jit(solution)/shard_map/all_to_all | solution.py:152
  97.6 194.4 %all-reduce.2.cloned.1.call-start = ((), (), s32[]{:S(2)}) async-start(), calls=%async_computation.2 | async-start | bytes 8388608 | tf_op jit(solution)/shard_map/psum | solution.py:178
  97.8 6.0 %copy-start.15 = (bf16[64,4,96]{2,1,0:T(4,128)(2,1)S(1)}, bf16[64,4,96]{2,1,0:T(4,128)(2,1)}, u32[]{:S(2)}) copy-start(bf16[64,4,96]{2,1,0:T(4,128)(2,1)} %copy-done.14) | copy-start | bytes 147460
  97.9 6.0 %slice-start.1 = ((s8[6291456]{0:T(1024)(128)(4,1)}), s8[4194304]{0:T(1024)(128)(4,1)S(1)}, s32[]{:S(2)}) async-start(s8[6291456]{0:T(1024)(128)(4,1)} %bitcast.102), calls=%async_computation.4 | async-start | bytes 8388608
  102.5 3.1 %copy-start.19 = (f32[512]{0:T(512)S(1)}, f32[512]{0:T(512)}, u32[]{:S(2)}) copy-start(f32[512]{0:T(512)} %param.16) | copy-start | bytes 6148
  102.5 3.1 %copy-start.22 = (f32[64]{0:T(128)S(1)}, f32[64]{0:T(128)}, u32[]{:S(2)}) copy-start(f32[64]{0:T(128)} %copy-done.21) | copy-start | bytes 772
  105.6 26.8 %copy-start.10 = (bf16[768,512]{1,0:T(8,128)(2,1)S(1)}, bf16[768,512]{1,0:T(8,128)(2,1)}, u32[]{:S(2)}) copy-start(bf16[768,512]{1,0:T(8,128)(2,1)} %copy-done.9) | copy-start | bytes 2359300
  132.4 1.3 copy-start.8
  132.4 1.8 copy-start.5
  136.6 0.7 copy-start.23
  136.6 0.7 copy-start.28
  136.6 4.9 %copy-start.4 = (bf16[2048,512]{0,1:T(8,128)(2,1)S(1)}, bf16[2048,512]{0,1:T(8,128)(2,1)}, u32[]{:S(2)}) copy-start(bf16[2048,512]{0,1:T(8,128)(2,1)} %copy-done.3) | copy-start | bytes 6291460
  136.6 4.9 %copy-start.25 = (s32[768]{0:T(1024)S(1)}, s32[768]{0:T(1024)}, u32[]{:S(2)}) copy-start(s32[768]{0:T(1024)} %copy-done.24) | copy-start | bytes 9220
  136.6 4.9 %copy-start.27 = (f32[512]{0:T(512)S(1)}, f32[512]{0:T(512)}, u32[]{:S(2)}) copy-start(f32[512]{0:T(512)} %param.15) | copy-start | bytes 6148
Sparse Core Ops, SparseCore 0:
  136.8 155.1 all-reduce.1
where the time goes:
time: 304 us; the launch traced here: 303 us
  waiting for transfers between devices  184 us (61%)
  matrix products  49.8 us (16%)
  local copies, waits for them, and re-layouts  25.1 us (8%)
  starting transfers between devices  21.8 us (7%)
  between operations  14.6 us (5%)
  other arithmetic  8.64 us (3%)
    psum x1, waiting for transfers between devices, shards(): weight_grads = lax.psum(local_grads, ('grid', 'sub'))  138 us
    all_to_all x1, waiting for transfers between devices, shards(): lax.all_to_all(home, 'sub', split_axis=1, concat_axis=1, tiled=True)  24.3 us
    unnamed x69, local copies, waits for them, and re-layouts  19.4 us
    all_to_all x1, waiting for transfers between devices, shards(): lax.all_to_all(packet, 'sub', split_axis=1, concat_axis=1, tiled=True)  17 us
    dot_general x1, matrix products, shards(): jnp.einsum('gjc,ce->gje', slot_onehot, recv_pair, preferred_element_type=...  11.4 us
    ppermute x4, starting transfers between devices, from_behind(): return lax.ppermute(block, axis, route)  10.8 us
    all_to_all x1, starting transfers between devices, shards(): lax.all_to_all(packet, 'sub', split_axis=1, concat_axis=1, tiled=True)  6.35 us
    dot_general x1, matrix products, shards(): jnp.einsum('sp,sd->pd', send_match.astype(jnp.float32), slot_back, precis...  6.08 us
  transfers between devices with their start and end apart: 7, of which 5 were waited for; matrix products, arithmetic and copies ran while one was open for 10% of the time, Pallas kernels for 0%

commit v1 on v0

--- a/solution.py
+++ b/solution.py
@@ -60,9 +60,15 @@
     )
     packet = sent_normed.reshape(3, sub_count, slots_per, model_width)
     packet_width = packet.shape[3]
-    mixed = lax.all_to_all(packet, "sub", split_axis=1, concat_axis=1, tiled=True).reshape(
-        3, block, packet_width
-    )
+    mixed = jnp.concatenate(
+        lax.all_to_all(
+            jnp.stack(jnp.split(packet, lax.axis_size("sub"), 1)),
+            axis_name="sub",
+            split_axis=0,
+            concat_axis=0,
+        ),
+        1,
+    ).reshape(3, block, packet_width)
     pieces = []
     for offset in (0, 1, 2):
         piece = mixed[offset]

time: 304 us -> 308 us (1.013)
    unnamed x69 -> x65, local copies, waits for them, and re-layouts: 19.4 us -> 19.4 us
where the time goes in v1:
time: 308 us; the launch traced here: 307 us
  waiting for transfers between devices  185 us (60%)
  matrix products  52.6 us (17%)
  local copies, waits for them, and re-layouts  25.1 us (8%)
  starting transfers between devices  20.2 us (7%)
  between operations  14.5 us (5%)
  other arithmetic  10.4 us (3%)
    psum x1, waiting for transfers between devices, shards(): weight_grads = lax.psum(local_grads, ('grid', 'sub'))  138 us
    all_to_all x1, waiting for transfers between devices, shards(): lax.all_to_all(home, 'sub', split_axis=1, concat_axis=1, tiled=True)  24.3 us
    unnamed x65, local copies, waits for them, and re-layouts  19.4 us
    all_to_all x1, waiting for transfers between devices, shards(): lax.all_to_all(jnp.stack(jnp.split(packet, lax.axis_size('sub'), 1)), axi...  18.1 us
    dot_general x1, matrix products, shards(): jnp.einsum('gjc,ce->gje', slot_onehot, recv_pair, preferred_element_type=...  11.4 us
    ppermute x4, starting transfers between devices, from_behind(): return lax.ppermute(block, axis, route)  9.18 us
    all_to_all x1, starting transfers between devices, shards(): lax.all_to_all(jnp.stack(jnp.split(packet, lax.axis_size('sub'), 1)), axi...  6.34 us
  transfers between devices with their start and end apart: 7, of which 5 were waited for; matrix products, arithmetic and copies ran while one was open for 10% of the time, Pallas kernels for 0%

profile of v1, /device:TPU:0, one launch (start us, length us, event | category | flops | bytes accessed | tf_op | source)
XLA Modules:
  0.0 307.5 jit_solution(14866794466971552783)
XLA Ops:
  7.2 3.0 copy.33
  10.2 0.5 fusion.22
  10.8 2.0 fusion.35
  12.8 0.9 copy-done.8
  13.7 1.0 pad_maximum_fusion.2
  14.7 6.3 %all-to-all-start = ((bf16[4,3,1,64,512]{4,3,1,2,0:T(8,128)(2,1)}), bf16[4,3,1,64,512]{4,3,1,2,0:T(8,128)(2,1)S(1)}, u32[]{:S(2)}, u32[]{:S(2)}) async-start(bf16[4,3,1,64,512]{4,3,1,2,0:T(8,128)(2,1)} %pad_maximum_fusion.2), calls=%async_computation | async-start | bytes 1572864 | tf_op jit(solution)/shard_map/all_to_all | solution.py:64
  21.2 0.9 constant_dynamic-update-slice_fusion.1
  22.0 0.5 multiply_multiply_fusion.1
  23.1 18.1 %all-to-all-done = bf16[4,3,1,64,512]{4,3,1,2,0:T(8,128)(2,1)S(1)} async-done(((bf16[4,3,1,64,512]{4,3,1,2,0:T(8,128)(2,1)}), bf16[4,3,1,64,512]{4,3,1,2,0:T(8,128)(2,1)S(1)}, u32[]{:S(2)}, u32[]{:S(2)}) %all-to-all-start) | async-done | bytes 786464 | tf_op jit(solution)/shard_map/all_to_all | solution.py:64
  41.2 1.3 collective-permute-start
  42.5 3.2 %collective-permute-start.1 = (bf16[256,512]{1,0:T(8,128)(2,1)S(1)}, bf16[256,512]{1,0:T(8,128)(2,1)S(1)}, u32[]{:S(2)}, u32[]{:S(2)}) collective-permute-start(bf16[256,512]{1,0:T(8,128)(2,1)S(1)} %bitcast.135), channel_id=1, source_target_pairs={{0,4},{4,8},{8,12},{12,16},{16,20},{20,24},{24,28},{1,5},{5,9},{9,... | collective-permute-start | bytes 786440 | tf_op jit(solution)/shard_map/ppermute | solution.py:13
  45.8 0.9 constant_dynamic-update-slice_fusion
  46.7 1.0 reshape.111
  47.7 0.8 broadcast_compare_fusion
  48.5 2.2 fusion.123
  50.7 11.4 %fusion.7 = bf16[64,96,1024]{2,1,0:T(8,128)(2,1)S(1)} fusion(s32[64,96]{1,0:T(8,128)} %param.22, bf16[768,1024,1]{1,0,2:T(8,128)(2,1)S(1)} %fusion.123), kind=kOutput, calls=%fused_computation.12 | convolution fusion | flops 9674686464 | bytes 14180352 | tf_op jit(solution)/shard_map/gjc,ce->gje/dot_general | solution.py:83
  62.2 4.9 %slice_bitcast_fusion.1 = (bf16[64,12,4,8,128]{4,3,2,1,0:T(8,128)(2,1)S(1)}, bf16[64,12,4,8,128]{4,3,2,1,0:T(8,128)(2,1)}) fusion(bf16[64,96,1024]{2,1,0:T(8,128)(2,1)S(1)} %fusion.7), kind=kLoop, calls=%fused_computation.22 | loop fusion | bytes 25165824
  67.1 3.3 %fusion.14 = f32[64,4,1,96]{3,2,1,0:T(1,128)S(1)} fusion(bf16[64,4,128,1]{2,3,1,0:T(2,128)(2,1)S(1)} %reshape.127, bf16[64,12,4,8,128]{4,3,2,1,0:T(8,128)(2,1)S(1)} %get-tuple-element.16), kind=kOutput, calls=%fused_computation.19 | convolution fusion | flops 6291456 | bytes 6455296 | tf_op jit(solution)/shard_map/gip,gjip->gij/dot_general | solution.py:93
  70.7 3.6 %fusion.39 = bf16[64,4,768]{2,1,0:T(4,128)(2,1)S(1)} fusion(s32[64,96]{1,0:T(8,128)S(1)} %copy-done.27, f32[64,4,96]{2,1,0:T(4,128)S(1)} %get-tuple-element.37, f32[64,4]{1,0:T(8,128)S(1)} %get-tuple-element.36), kind=kOutput, calls=%fused_computation.55 | convolution fusion | flops 42713088 | bytes 517120 | tf_op jit(solution)/shard_map/gij,gjc->gic/dot_general | solution.py:136
  74.3 0.4 convolution_convert_fusion.1
  75.0 6.1 %fusion.8 = f32[64,4,1,96]{3,2,1,0:T(1,128)S(1)} fusion(bf16[64,4,128,1]{2,3,1,0:T(2,128)(2,1)S(1)} %reshape.129, bf16[64,12,4,8,128]{4,3,2,1,0:T(8,128)(2,1)} %get-tuple-element.17), kind=kOutput, calls=%fused_computation.13 | convolution fusion | flops 6291456 | bytes 6455296 | tf_op jit(solution)/shard_map/gip,gjip->gij/dot_general | solution.py:116
  81.4 0.8 multiply_convert_fusion.1
  82.2 3.5 %fusion.38 = bf16[64,4,768]{2,1,0:T(4,128)(2,1)S(1)} fusion(bf16[64,4,96]{2,1,0:T(4,128)(2,1)S(1)} %get-tuple-element.30, s32[64,96]{1,0:T(8,128)S(1)} %copy-done.27), kind=kOutput, calls=%fused_computation.54 | convolution fusion | flops 42663936 | bytes 466944 | tf_op jit(solution)/shard_map/gij,gjc->gic/dot_general | solution.py:133
  85.7 0.4 convolution_convert_fusion.2
  86.6 3.4 %collective-permute-start.2 = (bf16[256,1024]{1,0:T(8,128)(2,1)S(1)}, bf16[256,1024]{1,0:T(8,128)(2,1)S(1)}, u32[]{:S(2)}, u32[]{:S(2)}) collective-permute-start(bf16[256,1024]{1,0:T(8,128)(2,1)S(1)} %get-tuple-element.20), channel_id=1, source_target_pairs={{0,4},{4,8},{8,12},{12,16},{16,20},{20,24},{24,28},{1,5},{5,9},{9,... | collective-permute-start | bytes 1572872 | tf_op jit(solution)/shard_map/ppermute | solution.py:13
  90.0 1.3 collective-permute-start.3
  91.5 4.3 %collective-permute-done.3 = bf16[256,1024]{1,0:T(8,128)(2,1)S(1)} collective-permute-done((bf16[256,1024]{1,0:T(8,128)(2,1)S(1)}, bf16[256,1024]{1,0:T(8,128)(2,1)S(1)}, u32[]{:S(2)}, u32[]{:S(2)}) %collective-permute-start.3) | collective-permute-done | bytes 524320 | tf_op jit(solution)/shard_map/ppermute | solution.py:13
  95.9 1.3 copy.43
  97.2 4.4 %all-to-all-start.1 = ((bf16[3,4,64,1024]{3,2,0,1:T(8,128)(2,1)}), bf16[3,4,64,1024]{3,2,0,1:T(8,128)(2,1)}, u32[]{:S(2)}, u32[]{:S(2)}) async-start(bf16[3,4,64,1024]{3,2,0,1:T(8,128)(2,1)} %copy.43), calls=%async_computation.1 | async-start | bytes 3145728 | tf_op jit(solution)/shard_map/all_to_all | solution.py:158
  101.9 4.7 %fusion.10 = f32[64,4,1,128]{3,2,1,0:T(1,128)S(1)} fusion(bf16[64,12,4,8,128]{4,3,2,1,0:T(8,128)(2,1)} %get-tuple-element.17, bf16[64,4,96,1]{2,1,0,3:T(4,128)(2,1)S(1)} %copy-done.15), kind=kOutput, calls=%fused_computation.15 | convolution fusion | flops 6291456 | bytes 6471680 | tf_op jit(solution)/shard_map/gij,gjik->gik/dot_general | solution.py:102
  106.6 1.3 convolution_bitcast_fusion
  107.9 1.7 fusion.12
  109.7 0.4 convolution_bitcast_fusion.1
  110.1 0.4 fusion.67
  110.5 24.3 %all-to-all-done.1 = bf16[3,4,64,1024]{3,2,0,1:T(8,128)(2,1)} async-done(((bf16[3,4,64,1024]{3,2,0,1:T(8,128)(2,1)}), bf16[3,4,64,1024]{3,2,0,1:T(8,128)(2,1)}, u32[]{:S(2)}, u32[]{:S(2)}) %all-to-all-start.1) | async-done | bytes 1572896 | tf_op jit(solution)/shard_map/all_to_all | solution.py:158
  134.8 1.6 copy.44
  136.4 1.0 fusion.94
  137.7 0.6 copy-done.4
  138.2 2.5 pad_maximum_fusion
  140.7 0.6 copy-done.21
  141.3 0.7 fusion.66
  142.0 0.8 fusion.44
  142.8 2.7 fusion.93
  145.6 6.1 %fusion.28 = (f32[2048]{0:T(1024)S(1)}, f32[2048,512]{0,1:T(8,128)S(1)}) fusion(bf16[2048,512]{0,1:T(8,128)(2,1)S(1)} %copy-done.3, f32[512]{0:T(512)S(1)} %copy-done.25, f32[768,512]{1,0:T(8,128)S(1)} %fusion.93, s32[768]{0:T(1024)S(1)} %copy-done.23), kind=kOutput, calls=%fused_computation.36 | convolution fusion | flops 9669441536 | bytes 7877632 | tf_op jit(solution)/shard_map/sp,sd->pd/dot_general | solution.py:163
  151.7 2.6 fusion.27
  154.3 3.9 %copy.45 = bf16[2048,512]{1,0:T(8,128)(2,1)} copy(bf16[2048,512]{0,1:T(8,128)(2,1)} %fusion.27) | data formatting | bytes 4194304
  158.2 137.8 %all-reduce.2.cloned.1.call-done = f32[4,512,512]{2,1,0:T(8,128)} async-done(((f32[4,512,512]{2,1,0:T(8,128)}), f32[4,512,512]{2,1,0:T(8,128)}) %all-reduce.2.cloned.1.call-update) | async-done | bytes 4194320 | tf_op jit(solution)/shard_map/psum | solution.py:184
  296.0 4.6 %copy.117 = f32[4,512,512]{2,1,0:T(8,128)} copy(f32[4,512,512]{2,1,0:T(8,128)} %all-reduce.2.cloned.1.call-done) | data formatting | bytes 8388608
  (83 shorter events, 3.2 us)
Async XLA Ops:
  7.2 15.7 %copy-start = (bf16[512,512]{1,0:T(8,128)(2,1)S(1)}, bf16[512,512]{1,0:T(8,128)(2,1)}, u32[]{:S(2)}) copy-start(bf16[512,512]{1,0:T(8,128)(2,1)} %param.17) | copy-start | bytes 1572868
  7.2 3.5 %copy-start.18 = (s32[1,3,4,64]{3,2,1,0:T(4,128)S(1)}, s32[1,3,4,64]{3,2,1,0:T(4,128)}, u32[]{:S(2)}) copy-start(s32[1,3,4,64]{3,2,1,0:T(4,128)} %param.24) | copy-start | bytes 9220
  7.2 3.6 %copy-start.24 = (f32[512]{0:T(512)S(1)}, f32[512]{0:T(512)}, u32[]{:S(2)}) copy-start(f32[512]{0:T(512)} %param.15) | copy-start | bytes 6148
  10.2 2.5 copy-start.2
  10.8 2.0 copy-start.22
  12.7 0.9 copy-start.8
  12.8 8.3 %copy-start.5 = (bf16[64,512]{1,0:T(8,128)(2,1)S(1)}, bf16[64,512]{1,0:T(8,128)(2,1)}, u32[]{:S(2)}) copy-start(bf16[64,512]{1,0:T(8,128)(2,1)} %param.14) | copy-start | bytes 196612
  12.8 9.8 %copy-start.6 = (bf16[512,512]{1,0:T(8,128)(2,1)S(1)}, bf16[512,512]{1,0:T(8,128)(2,1)}, u32[]{:S(2)}) copy-start(bf16[512,512]{1,0:T(8,128)(2,1)} %param.20) | copy-start | bytes 1572868
  12.8 9.8 %copy-start.10 = (bf16[64,512]{1,0:T(8,128)(2,1)S(1)}, bf16[64,512]{1,0:T(8,128)(2,1)}, u32[]{:S(2)}) copy-start(bf16[64,512]{1,0:T(8,128)(2,1)} %param.25) | copy-start | bytes 196612
  13.7 7.5 %copy-start.11 = (bf16[512,512]{1,0:T(8,128)(2,1)S(1)}, bf16[512,512]{1,0:T(8,128)(2,1)}, u32[]{:S(2)}) copy-start(bf16[512,512]{1,0:T(8,128)(2,1)} %param.18) | copy-start | bytes 1572868
  13.7 9.2 %copy-start.16 = (f32[512]{0:T(512)S(1)}, f32[512]{0:T(512)}, u32[]{:S(2)}) copy-start(f32[512]{0:T(512)} %param.16) | copy-start | bytes 6148
  13.7 32.1 %copy-start.12 = (bf16[512,512]{1,0:T(8,128)(2,1)S(1)}, bf16[512,512]{1,0:T(8,128)(2,1)}, u32[]{:S(2)}) copy-start(bf16[512,512]{1,0:T(8,128)(2,1)} %param.19) | copy-start | bytes 1572868
  14.7 26.5 %all-to-all-start = ((bf16[4,3,1,64,512]{4,3,1,2,0:T(8,128)(2,1)}), bf16[4,3,1,64,512]{4,3,1,2,0:T(8,128)(2,1)S(1)}, u32[]{:S(2)}, u32[]{:S(2)}) async-start(bf16[4,3,1,64,512]{4,3,1,2,0:T(8,128)(2,1)} %pad_maximum_fusion.2), calls=%async_computation | async-start | bytes 1572864 | tf_op jit(solution)/shard_map/all_to_all | solution.py:64
  22.5 18.6 %copy-start.19 = (f32[64]{0:T(128)}, f32[64]{0:T(128)S(1)}, u32[]{:S(2)}) copy-start(f32[64]{0:T(128)S(1)} %get-tuple-element.35) | copy-start | bytes 772
  41.2 7.3 %collective-permute-start = (bf16[256,512]{1,0:T(8,128)(2,1)S(1)}, bf16[256,512]{1,0:T(8,128)(2,1)S(1)}, u32[]{:S(2)}, u32[]{:S(2)}) collective-permute-start(bf16[256,512]{1,0:T(8,128)(2,1)S(1)} %bitcast.136), channel_id=1, source_target_pairs={{4,0},{8,4},{12,8},{16,12},{20,16},{24,20},{28,24},{5,1},{9,5},{13... | collective-permute-start | bytes 786440 | tf_op jit(solution)/shard_map/ppermute | solution.py:13
  42.5 6.0 %collective-permute-start.1 = (bf16[256,512]{1,0:T(8,128)(2,1)S(1)}, bf16[256,512]{1,0:T(8,128)(2,1)S(1)}, u32[]{:S(2)}, u32[]{:S(2)}) collective-permute-start(bf16[256,512]{1,0:T(8,128)(2,1)S(1)} %bitcast.135), channel_id=1, source_target_pairs={{0,4},{4,8},{8,12},{12,16},{16,20},{20,24},{24,28},{1,5},{5,9},{9,... | collective-permute-start | bytes 786440 | tf_op jit(solution)/shard_map/ppermute | solution.py:13
  67.1 7.2 %copy-start.1 = (bf16[64,12,4,8,128]{4,3,2,1,0:T(8,128)(2,1)}, bf16[64,12,4,8,128]{4,3,2,1,0:T(8,128)(2,1)S(1)}, u32[]{:S(2)}) copy-start(bf16[64,12,4,8,128]{4,3,2,1,0:T(8,128)(2,1)S(1)} %get-tuple-element.16) | copy-start | bytes 18874372
  67.1 3.6 %copy-start.27 = (s32[64,96]{1,0:T(8,128)S(1)}, s32[64,96]{1,0:T(8,128)}, u32[]{:S(2)}) copy-start(s32[64,96]{1,0:T(8,128)} %param.22) | copy-start | bytes 73732
  82.2 4.0 %copy-start.13 = (bf16[64,4,96]{2,1,0:T(4,128)(2,1)}, bf16[64,4,96]{2,1,0:T(4,128)(2,1)S(1)}, u32[]{:S(2)}) copy-start(bf16[64,4,96]{2,1,0:T(4,128)(2,1)S(1)} %get-tuple-element.30) | copy-start | bytes 147460
  86.6 4.9 %collective-permute-start.2 = (bf16[256,1024]{1,0:T(8,128)(2,1)S(1)}, bf16[256,1024]{1,0:T(8,128)(2,1)S(1)}, u32[]{:S(2)}, u32[]{:S(2)}) collective-permute-start(bf16[256,1024]{1,0:T(8,128)(2,1)S(1)} %get-tuple-element.20), channel_id=1, source_target_pairs={{0,4},{4,8},{8,12},{12,16},{16,20},{20,24},{24,28},{1,5},{5,9},{9,... | collective-permute-start | bytes 1572872 | tf_op jit(solution)/shard_map/ppermute | solution.py:13
  90.0 5.8 %collective-permute-start.3 = (bf16[256,1024]{1,0:T(8,128)(2,1)S(1)}, bf16[256,1024]{1,0:T(8,128)(2,1)S(1)}, u32[]{:S(2)}, u32[]{:S(2)}) collective-permute-start(bf16[256,1024]{1,0:T(8,128)(2,1)S(1)} %get-tuple-element.21), channel_id=1, source_target_pairs={{4,0},{8,4},{12,8},{16,12},{20,16},{24,20},{28,24},{5,1},{9,5},{13... | collective-permute-start | bytes 1572872 | tf_op jit(solution)/shard_map/ppermute | solution.py:13
  95.7 6.2 %copy-start.15 = (bf16[64,4,96,1]{2,1,0,3:T(4,128)(2,1)S(1)}, bf16[64,4,96,1]{2,1,0,3:T(4,128)(2,1)}, u32[]{:S(2)}) copy-start(bf16[64,4,96,1]{2,1,0,3:T(4,128)(2,1)} %get-tuple-element.31) | copy-start | bytes 147460
  95.9 12.0 %slice-start = ((s8[6291456]{0:T(1024)(128)(4,1)}), s8[2097152]{0:T(1024)(128)(4,1)S(1)}, s32[]{:S(2)}) async-start(s8[6291456]{0:T(1024)(128)(4,1)} %bitcast.117), calls=%async_computation.3 | async-start | bytes 4194304
  97.2 37.6 %all-to-all-start.1 = ((bf16[3,4,64,1024]{3,2,0,1:T(8,128)(2,1)}), bf16[3,4,64,1024]{3,2,0,1:T(8,128)(2,1)}, u32[]{:S(2)}, u32[]{:S(2)}) async-start(bf16[3,4,64,1024]{3,2,0,1:T(8,128)(2,1)} %copy.43), calls=%async_computation.1 | async-start | bytes 3145728 | tf_op jit(solution)/shard_map/all_to_all | solution.py:158
  101.6 194.4 %all-reduce.2.cloned.1.call-start = ((), (), s32[]{:S(2)}) async-start(), calls=%async_computation.2 | async-start | bytes 8388608 | tf_op jit(solution)/shard_map/psum | solution.py:184
  101.9 6.0 %copy-start.14 = (bf16[64,4,96]{2,1,0:T(4,128)(2,1)S(1)}, bf16[64,4,96]{2,1,0:T(4,128)(2,1)}, u32[]{:S(2)}) copy-start(bf16[64,4,96]{2,1,0:T(4,128)(2,1)} %copy-done.13) | copy-start | bytes 147460
  101.9 6.0 %slice-start.1 = ((s8[6291456]{0:T(1024)(128)(4,1)}), s8[4194304]{0:T(1024)(128)(4,1)S(1)}, s32[]{:S(2)}) async-start(s8[6291456]{0:T(1024)(128)(4,1)} %bitcast.117), calls=%async_computation.4 | async-start | bytes 8388608
  106.6 3.1 %copy-start.17 = (f32[512]{0:T(512)S(1)}, f32[512]{0:T(512)}, u32[]{:S(2)}) copy-start(f32[512]{0:T(512)} %param.16) | copy-start | bytes 6148
  106.6 3.1 %copy-start.20 = (f32[64]{0:T(128)S(1)}, f32[64]{0:T(128)}, u32[]{:S(2)}) copy-start(f32[64]{0:T(128)} %copy-done.19) | copy-start | bytes 772
  109.6 26.8 %copy-start.9 = (bf16[768,512]{1,0:T(8,128)(2,1)S(1)}, bf16[768,512]{1,0:T(8,128)(2,1)}, u32[]{:S(2)}) copy-start(bf16[768,512]{1,0:T(8,128)(2,1)} %copy-done.8) | copy-start | bytes 2359300
  136.4 1.3 copy-start.7
  136.4 1.8 copy-start.4
  140.7 0.6 copy-start.21
  140.7 0.6 copy-start.26
  140.7 4.9 %copy-start.3 = (bf16[2048,512]{0,1:T(8,128)(2,1)S(1)}, bf16[2048,512]{0,1:T(8,128)(2,1)}, u32[]{:S(2)}) copy-start(bf16[2048,512]{0,1:T(8,128)(2,1)} %copy-done.2) | copy-start | bytes 6291460
  140.7 4.9 %copy-start.23 = (s32[768]{0:T(1024)S(1)}, s32[768]{0:T(1024)}, u32[]{:S(2)}) copy-start(s32[768]{0:T(1024)} %copy-done.22) | copy-start | bytes 9220
  140.7 4.9 %copy-start.25 = (f32[512]{0:T(512)S(1)}, f32[512]{0:T(512)}, u32[]{:S(2)}) copy-start(f32[512]{0:T(512)} %param.15) | copy-start | bytes 6148
Sparse Core Ops, SparseCore 0:
  140.8 155.0 all-reduce.1
